TPU v7x, 32 devices: a whole 2x2x4 slice. The times are simulated.
32 devices in a mesh: group: 2 (over y), col: 4 (over z), row: 2 (over x), section: 2 (over core).
Axes of the slice: x: 2, y: 2, z: 4, core: 2. Of those that a mesh axis runs over, the one named last changes fastest.
Arguments:
- tokens: bfloat16 [2, 256, 8192], P(None, ('group', 'col'), 'row'), parts along dimension 1, may hold values from -12 to 12, as said below
- norm_gain: float32 [2, 8192], P('section', 'row'), may hold values from 0.5 to 1.5
- w_gate: bfloat16 [2, 8192, 14336], P('section', 'row', 'col'), may hold values from -0.0625 to 0.0625
- w_up: bfloat16 [2, 8192, 14336], P('section', 'row', 'col'), may hold values from -0.0625 to 0.0625
- w_down: bfloat16 [2, 14336, 8192], P('section', 'col', 'row'), may hold values from -0.046875 to 0.046875
Outputs:
- block_out: bfloat16 [2, 2, 256, 8192], P('section', None, ('group', 'col'), 'row'), parts along dimension 2
There are 2 independent parts, one for each index of `group`. A program takes and returns all parts, laid end to end along the dimension named above; an argument that names none is the same for every part. Nothing has to cross between parts.
Inputs may be any that keep to these rules, and one draw needn't show every extreme that they name: `tokens`: dense real activations.
All inputs are finite; a program needn't handle non-finite values.
Results may differ from a plain program's by a relative error of at most 0.024.
Values may be sent and summed in bfloat16 or wider, within the bound.
A program may use at most 128 MiB of HBM per device.

v0:
```python
import jax
import jax.numpy as jnp
from jax import lax
from jax.sharding import PartitionSpec as P

D = 8192
EPS = 1e-05


def from_behind(value, axis, steps):
    count = lax.axis_size(axis)
    initial, last = (max(0, -steps), min(count, count - steps))
    return lax.ppermute(value, axis, [(source, source + steps) for source in range(initial, last)])


def on_device(tokens, norm_gain, w_gate, w_up, w_down):
    section_index = lax.axis_index("section")
    is_first = section_index == 0
    gain = norm_gain[0]
    gate_tile = w_gate[0]
    up_tile = w_up[0]
    down_tile = w_down[0]
    micro, tok_col, width_row = tokens.shape
    hidden_cols = gate_tile.shape[1]
    results = []
    received = jnp.zeros((tok_col, width_row), jnp.bfloat16)
    for tick in range(micro + 1):
        fresh = tokens[tick] if tick < micro else jnp.zeros((tok_col, width_row), jnp.bfloat16)
        block_in = jnp.where(is_first, fresh, received)
        wide_in = block_in.astype(jnp.float32)
        sum_sq = lax.psum(jnp.sum(wide_in * wide_in, axis=1), "row")
        wide = block_in.astype(jnp.float32)
        scale = lax.rsqrt(sum_sq / D + EPS)
        normed = (wide * scale[:, None] * gain[None, :]).astype(jnp.bfloat16)
        normed_rows = lax.all_gather(normed, "col", axis=0, tiled=True)
        gate_part = jnp.dot(normed_rows, gate_tile, preferred_element_type=jnp.float32)
        up_part = jnp.dot(normed_rows, up_tile, preferred_element_type=jnp.float32)
        pair = jnp.concatenate([gate_part, up_part], axis=1)
        share = lax.psum_scatter(
            pair.astype(jnp.bfloat16), "row", scatter_dimension=0, tiled=True
        ).astype(jnp.float32)
        hidden_share = (jax.nn.silu(share[:, :hidden_cols]) * share[:, hidden_cols:]).astype(
            jnp.bfloat16
        )
        hidden = lax.all_gather(hidden_share, "row", axis=0, tiled=True)
        ffn = lax.psum_scatter(
            jnp.dot(hidden, down_tile, preferred_element_type=jnp.float32).astype(jnp.bfloat16),
            "col",
            scatter_dimension=0,
            tiled=True,
        ).astype(jnp.float32)
        result = (wide_in + ffn).astype(jnp.bfloat16)
        results.append(result)
        if tick < micro:
            received = from_behind(result, "section", 1)
    early = jnp.stack(results[:micro], axis=0)
    late = jnp.stack(results[1:], axis=0)
    return jnp.where(is_first, early, late)[None]


def solution(mesh):
    placed = (
        P(None, ("group", "col"), "row"),
        P("section", "row"),
        P("section", "row", "col"),
        P("section", "row", "col"),
        P("section", "col", "row"),
    )
    return jax.shard_map(
        on_device,
        mesh=mesh,
        in_specs=placed,
        out_specs=P("section", None, ("group", "col"), "row"),
        check_vma=False,
    )
```

profile of v0, /device:TPU:0, one launch (start us, length us, event | category | flops | bytes accessed | tf_op | source)
XLA Modules:
  0.0 455.9 jit_solution(14409287867418705781)
XLA Ops:
  7.7 5.9 %psum.21 = f32[32]{0:T(128)S(1)} all-reduce(f32[32]{0:T(128)S(1)} %fusion.56), channel_id=1, replica_groups=mesh['group'=2,'col'=4,'row'=2,'section'=2] {'row'}, use_global_device_ids=true, to_apply=%region_1.2 | all-reduce | flops 32 | bytes 256 | tf_op jit(solution)/shard_map/psum | solution.py:31
  13.5 1.8 fusion.58
  15.4 29.9 %all-gather.4.cloned.1.call-done = bf16[128,4096]{1,0:T(8,128)(2,1)} async-done(((bf16[32,4096]{1,0:T(8,128)(2,1)}), bf16[128,4096]{1,0:T(8,128)(2,1)}) %all-gather.4.cloned.1.call-update) | async-done | bytes 1048592 | tf_op jit(solution)/shard_map/all_gather | solution.py:35
  45.3 13.7 %fusion.27 = bf16[128,3584]{1,0:T(8,128)(2,1)S(1)} fusion(bf16[128,4096]{1,0:T(8,128)(2,1)} %all-gather.4.cloned.1.call-done, bf16[1,4096,3584]{2,1,0:T(8,128)(2,1)} %param.8), kind=kOutput, calls=%fused_computation.21 | convolution fusion | flops 3758555136 | bytes 31326208 | tf_op jit(solution)/shard_map/dot_general | solution.py:37
  59.0 11.6 %fusion.18 = bf16[128,3584]{1,0:T(8,128)(2,1)S(1)} fusion(bf16[128,4096]{1,0:T(8,128)(2,1)S(1)} %copy-done, bf16[1,4096,3584]{2,1,0:T(8,128)(2,1)} %param.7), kind=kOutput, calls=%fused_computation.18 | convolution fusion | flops 3758555136 | bytes 31326208 | tf_op jit(solution)/shard_map/dot_general | solution.py:36
  70.6 1.4 pad_maximum_fusion
  72.1 28.5 %reduce-scatter.7.cloned.1.call-done = bf16[64,7168]{1,0:T(8,128)(2,1)} async-done(((bf16[128,7168]{1,0:T(8,128)(2,1)}), bf16[64,7168]{1,0:T(8,128)(2,1)}) %reduce-scatter.7.cloned.1.call-update) | async-done | bytes 917520 | tf_op jit(solution)/shard_map/reduce_scatter | solution.py:39
  100.6 1.3 convert_element_type.75
  102.2 12.8 %all_gather.19 = bf16[128,3584]{1,0:T(8,128)(2,1)S(1)} all-gather(bf16[64,3584]{1,0:T(8,128)(2,1)S(1)} %fusion.47), channel_id=1, replica_groups=mesh['group'=2,'col'=4,'row'=2,'section'=2] {'row'}, dimensions={0}, use_global_device_ids=true | all-gather | bytes 1376256 | tf_op jit(solution)/shard_map/all_gather | solution.py:45
  115.0 12.6 %fusion.36 = bf16[128,4096]{1,0:T(8,128)(2,1)} fusion(bf16[128,3584]{1,0:T(8,128)(2,1)S(1)} %all_gather.19, bf16[1,3584,4096]{2,1,0:T(8,128)(2,1)} %param.9), kind=kOutput, calls=%fused_computation.24 | convolution fusion | flops 3758620672 | bytes 31326208 | tf_op jit(solution)/shard_map/dot_general | solution.py:47
  127.6 27.4 %reduce-scatter.9.cloned.1.call-done = bf16[32,4096]{1,0:T(8,128)(2,1)} async-done(((bf16[128,4096]{1,0:T(8,128)(2,1)}), bf16[32,4096]{1,0:T(8,128)(2,1)}) %reduce-scatter.9.cloned.1.call-update) | async-done | bytes 262160 | tf_op jit(solution)/shard_map/reduce_scatter | solution.py:46
  156.1 1.3 collective-permute-start
  158.8 4.9 %psum.22 = f32[32]{0:T(128)S(1)} all-reduce(f32[32]{0:T(128)S(1)} %get-tuple-element.5), channel_id=1, replica_groups=mesh['group'=2,'col'=4,'row'=2,'section'=2] {'row'}, use_global_device_ids=true, to_apply=%region_5.6 | all-reduce | flops 32 | bytes 256 | tf_op jit(solution)/shard_map/psum | solution.py:31
  164.8 26.8 %all-gather.6.cloned.1.call-done = bf16[128,4096]{1,0:T(8,128)(2,1)} async-done(((bf16[32,4096]{1,0:T(8,128)(2,1)}), bf16[128,4096]{1,0:T(8,128)(2,1)}) %all-gather.6.cloned.1.call-update) | async-done | bytes 1048592 | tf_op jit(solution)/shard_map/all_gather | solution.py:35
  191.6 13.7 %fusion.30 = bf16[128,3584]{1,0:T(8,128)(2,1)S(1)} fusion(bf16[128,4096]{1,0:T(8,128)(2,1)} %all-gather.6.cloned.1.call-done, bf16[1,4096,3584]{2,1,0:T(8,128)(2,1)} %param.8), kind=kOutput, calls=%fused_computation.22 | convolution fusion | flops 3758555136 | bytes 31326208 | tf_op jit(solution)/shard_map/dot_general | solution.py:37
  205.3 11.6 %fusion.21 = bf16[128,3584]{1,0:T(8,128)(2,1)S(1)} fusion(bf16[128,4096]{1,0:T(8,128)(2,1)S(1)} %copy-done.1, bf16[1,4096,3584]{2,1,0:T(8,128)(2,1)} %param.7), kind=kOutput, calls=%fused_computation.19 | convolution fusion | flops 3758555136 | bytes 31326208 | tf_op jit(solution)/shard_map/dot_general | solution.py:36
  216.9 1.4 pad_maximum_fusion.1
  218.4 28.5 %reduce-scatter.11.cloned.1.call-done = bf16[64,7168]{1,0:T(8,128)(2,1)} async-done(((bf16[128,7168]{1,0:T(8,128)(2,1)}), bf16[64,7168]{1,0:T(8,128)(2,1)}) %reduce-scatter.11.cloned.1.call-update) | async-done | bytes 917520 | tf_op jit(solution)/shard_map/reduce_scatter | solution.py:39
  246.9 1.3 convert_element_type.82
  248.5 12.8 %all_gather.21 = bf16[128,3584]{1,0:T(8,128)(2,1)S(1)} all-gather(bf16[64,3584]{1,0:T(8,128)(2,1)S(1)} %fusion.46), channel_id=1, replica_groups=mesh['group'=2,'col'=4,'row'=2,'section'=2] {'row'}, dimensions={0}, use_global_device_ids=true | all-gather | bytes 1376256 | tf_op jit(solution)/shard_map/all_gather | solution.py:45
  261.2 12.5 %fusion.39 = bf16[128,4096]{1,0:T(8,128)(2,1)} fusion(bf16[128,3584]{1,0:T(8,128)(2,1)S(1)} %all_gather.21, bf16[1,3584,4096]{2,1,0:T(8,128)(2,1)} %param.9), kind=kOutput, calls=%fused_computation.25 | convolution fusion | flops 3758620672 | bytes 31326208 | tf_op jit(solution)/shard_map/dot_general | solution.py:47
  273.8 27.4 %reduce-scatter.13.cloned.1.call-done = bf16[32,4096]{1,0:T(8,128)(2,1)} async-done(((bf16[128,4096]{1,0:T(8,128)(2,1)}), bf16[32,4096]{1,0:T(8,128)(2,1)}) %reduce-scatter.13.cloned.1.call-update) | async-done | bytes 262160 | tf_op jit(solution)/shard_map/reduce_scatter | solution.py:46
  302.3 1.3 collective-permute-start.1
  304.9 4.9 %psum.23 = f32[32]{0:T(128)S(1)} all-reduce(f32[32]{0:T(128)S(1)} %fusion.52), channel_id=1, replica_groups=mesh['group'=2,'col'=4,'row'=2,'section'=2] {'row'}, use_global_device_ids=true, to_apply=%region_9.10 | all-reduce | flops 32 | bytes 256 | tf_op jit(solution)/shard_map/psum | solution.py:31
  311.0 26.7 %all-gather.8.cloned.1.call-done = bf16[128,4096]{1,0:T(8,128)(2,1)} async-done(((bf16[32,4096]{1,0:T(8,128)(2,1)}), bf16[128,4096]{1,0:T(8,128)(2,1)}) %all-gather.8.cloned.1.call-update) | async-done | bytes 1048592 | tf_op jit(solution)/shard_map/all_gather | solution.py:35
  337.7 13.7 %fusion.33 = bf16[128,3584]{1,0:T(8,128)(2,1)S(1)} fusion(bf16[128,4096]{1,0:T(8,128)(2,1)} %all-gather.8.cloned.1.call-done, bf16[1,4096,3584]{2,1,0:T(8,128)(2,1)} %param.8), kind=kOutput, calls=%fused_computation.23 | convolution fusion | flops 3758555136 | bytes 31326208 | tf_op jit(solution)/shard_map/dot_general | solution.py:37
  351.5 11.6 %fusion.24 = bf16[128,3584]{1,0:T(8,128)(2,1)S(1)} fusion(bf16[128,4096]{1,0:T(8,128)(2,1)S(1)} %copy-done.2, bf16[1,4096,3584]{2,1,0:T(8,128)(2,1)} %param.7), kind=kOutput, calls=%fused_computation.20 | convolution fusion | flops 3758555136 | bytes 31326208 | tf_op jit(solution)/shard_map/dot_general | solution.py:36
  363.1 1.4 pad_maximum_fusion.2
  364.6 28.5 %reduce-scatter.15.cloned.1.call-done = bf16[64,7168]{1,0:T(8,128)(2,1)} async-done(((bf16[128,7168]{1,0:T(8,128)(2,1)}), bf16[64,7168]{1,0:T(8,128)(2,1)}) %reduce-scatter.15.cloned.1.call-update) | async-done | bytes 917520 | tf_op jit(solution)/shard_map/reduce_scatter | solution.py:39
  394.6 12.8 %all_gather.23 = bf16[128,3584]{1,0:T(8,128)(2,1)S(1)} all-gather(bf16[64,3584]{1,0:T(8,128)(2,1)S(1)} %fusion.45), channel_id=1, replica_groups=mesh['group'=2,'col'=4,'row'=2,'section'=2] {'row'}, dimensions={0}, use_global_device_ids=true | all-gather | bytes 1376256 | tf_op jit(solution)/shard_map/all_gather | solution.py:45
  407.4 12.5 %fusion.42 = bf16[128,4096]{1,0:T(8,128)(2,1)} fusion(bf16[128,3584]{1,0:T(8,128)(2,1)S(1)} %all_gather.23, bf16[1,3584,4096]{2,1,0:T(8,128)(2,1)} %param.9), kind=kOutput, calls=%fused_computation.26 | convolution fusion | flops 3758620672 | bytes 31326208 | tf_op jit(solution)/shard_map/dot_general | solution.py:47
  419.9 27.5 %reduce-scatter.17.cloned.1.call-done = bf16[32,4096]{1,0:T(8,128)(2,1)} async-done(((bf16[128,4096]{1,0:T(8,128)(2,1)}), bf16[32,4096]{1,0:T(8,128)(2,1)}) %reduce-scatter.17.cloned.1.call-update) | async-done | bytes 262160 | tf_op jit(solution)/shard_map/reduce_scatter | solution.py:46
  (46 shorter events, 12.4 us)
Async XLA Ops:
  6.5 38.8 %all-gather.4.cloned.1.call-start = ((), (), s32[]{:S(2)}) async-start(), calls=%async_computation.6 | async-start | bytes 1310720 | tf_op jit(solution)/shard_map/all_gather | solution.py:35
  15.4 85.3 %reduce-scatter.7.cloned.1.call-start = ((), (), s32[]{:S(2)}) async-start(), calls=%async_computation.7 | async-start | bytes 2752512 | tf_op jit(solution)/shard_map/reduce_scatter | solution.py:39
  45.3 13.7 %copy-start = (bf16[128,4096]{1,0:T(8,128)(2,1)S(1)}, bf16[128,4096]{1,0:T(8,128)(2,1)}, u32[]{:S(2)}) copy-start(bf16[128,4096]{1,0:T(8,128)(2,1)} %all-gather.4.cloned.1.call-done) | copy-start | bytes 3145732
  72.1 83.0 %reduce-scatter.9.cloned.1.call-start = ((), (), s32[]{:S(2)}) async-start(), calls=%async_computation.8 | async-start | bytes 1310720 | tf_op jit(solution)/shard_map/reduce_scatter | solution.py:46
  115.0 40.1 %copy-start.3 = (bf16[2,32,4096]{2,1,0:T(8,128)(2,1)S(1)}, bf16[2,32,4096]{2,1,0:T(8,128)(2,1)}, u32[]{:S(2)}) copy-start(bf16[2,32,4096]{2,1,0:T(8,128)(2,1)} %param.5) | copy-start | bytes 1572868
  115.0 48.8 %copy-start.4 = (f32[1,4096]{1,0:T(1,128)S(1)}, f32[1,4096]{1,0:T(1,128)}, u32[]{:S(2)}) copy-start(f32[1,4096]{1,0:T(1,128)} %param.6) | copy-start | bytes 49156
  127.6 64.0 %all-gather.6.cloned.1.call-start = ((), (), s32[]{:S(2)}) async-start(), calls=%async_computation.9 | async-start | bytes 1310720 | tf_op jit(solution)/shard_map/all_gather | solution.py:35
  156.1 2.5 collective-permute-start
  164.6 82.3 %reduce-scatter.11.cloned.1.call-start = ((), (), s32[]{:S(2)}) async-start(), calls=%async_computation.10 | async-start | bytes 2752512 | tf_op jit(solution)/shard_map/reduce_scatter | solution.py:39
  191.6 13.7 %copy-start.1 = (bf16[128,4096]{1,0:T(8,128)(2,1)S(1)}, bf16[128,4096]{1,0:T(8,128)(2,1)}, u32[]{:S(2)}) copy-start(bf16[128,4096]{1,0:T(8,128)(2,1)} %all-gather.6.cloned.1.call-done) | copy-start | bytes 3145732
  218.4 82.9 %reduce-scatter.13.cloned.1.call-start = ((), (), s32[]{:S(2)}) async-start(), calls=%async_computation.11 | async-start | bytes 1310720 | tf_op jit(solution)/shard_map/reduce_scatter | solution.py:46
  273.8 63.9 %all-gather.8.cloned.1.call-start = ((), (), s32[]{:S(2)}) async-start(), calls=%async_computation.12 | async-start | bytes 1310720 | tf_op jit(solution)/shard_map/all_gather | solution.py:35
  302.3 2.5 collective-permute-start.1
  310.7 82.3 %reduce-scatter.15.cloned.1.call-start = ((), (), s32[]{:S(2)}) async-start(), calls=%async_computation.13 | async-start | bytes 2752512 | tf_op jit(solution)/shard_map/reduce_scatter | solution.py:39
  337.7 13.7 %copy-start.2 = (bf16[128,4096]{1,0:T(8,128)(2,1)S(1)}, bf16[128,4096]{1,0:T(8,128)(2,1)}, u32[]{:S(2)}) copy-start(bf16[128,4096]{1,0:T(8,128)(2,1)} %all-gather.8.cloned.1.call-done) | copy-start | bytes 3145732
  364.5 82.9 %reduce-scatter.17.cloned.1.call-start = ((), (), s32[]{:S(2)}) async-start(), calls=%async_computation.14 | async-start | bytes 1310720 | tf_op jit(solution)/shard_map/reduce_scatter | solution.py:46
Sparse Core Ops, SparseCore 0:
  15.5 29.7 all-gather.3
  72.2 28.3 reduce-scatter.6
  127.7 27.3 reduce-scatter.8
  164.7 26.8 all-gather.5
  218.5 28.3 reduce-scatter.10
  273.9 27.3 reduce-scatter.12
  310.9 26.8 all-gather.7
  364.6 28.3 reduce-scatter.14
  420.1 27.3 reduce-scatter.16
where the time goes:
time: 456 us
  waiting for transfers between devices  254 us (56%)
  matrix products  114 us (25%)
  blocking collectives  54 us (12%)
  other arithmetic  17.9 us (4%)
  between operations  13.4 us (3%)
    reduce_scatter x3, waiting for transfers between devices, on_device(): lax.psum_scatter(pair.astype(jnp.bfloat16), 'row', scatter_dimension=0, t...  85.5 us
    all_gather x3, waiting for transfers between devices, on_device(): normed_rows = lax.all_gather(normed, 'col', axis=0, tiled=True)  83.4 us
    reduce_scatter x3, waiting for transfers between devices, on_device(): lax.psum_scatter(jnp.dot(hidden, down_tile, preferred_element_type=jnp.fl...  82.3 us
    dot_general x3, matrix products, on_device(): up_part = jnp.dot(normed_rows, up_tile, preferred_element_type=jnp.float32)  41.2 us
    all_gather x3, blocking collectives, on_device(): hidden = lax.all_gather(hidden_share, 'row', axis=0, tiled=True)  38.3 us
    dot_general x3, matrix products, on_device(): jnp.dot(hidden, down_tile, preferred_element_type=jnp.float32)  37.7 us
    dot_general x3, matrix products, on_device(): jnp.dot(normed_rows, gate_tile, preferred_element_type=jnp.float32)  34.8 us
    psum x3, blocking collectives, on_device(): sum_sq = lax.psum(jnp.sum(wide_in * wide_in, axis=1), 'row')  15.7 us
  transfers between devices with their start and end apart: 11, of which 11 were waited for; matrix products, arithmetic and copies ran while one was open for 0% of the time, Pallas kernels for 0%

commit v1 on v0

--- a/solution.py
+++ b/solution.py
@@ -32,7 +32,16 @@
         wide = block_in.astype(jnp.float32)
         scale = lax.rsqrt(sum_sq / D + EPS)
         normed = (wide * scale[:, None] * gain[None, :]).astype(jnp.bfloat16)
-        normed_rows = lax.all_gather(normed, "col", axis=0, tiled=True)
+        shard = normed
+        ways, here, hop = (lax.axis_size("col"), lax.axis_index("col"), shard.shape[0])
+        shape = [n * ways if d == 0 else n for d, n in enumerate(shard.shape)]
+        full = lax.dynamic_update_slice_in_dim(
+            jnp.zeros(shape, shard.dtype), shard, here * hop, axis=0
+        )
+        for far in range(1, ways):
+            shard = lax.ppermute(shard, "col", [(d, (d + 1) % ways) for d in range(ways)])
+            full = lax.dynamic_update_slice_in_dim(full, shard, (here - far) % ways * hop, axis=0)
+        normed_rows = full
         gate_part = jnp.dot(normed_rows, gate_tile, preferred_element_type=jnp.float32)
         up_part = jnp.dot(normed_rows, up_tile, preferred_element_type=jnp.float32)
         pair = jnp.concatenate([gate_part, up_part], axis=1)

time: 456 us -> 438 us (0.961)
  waiting for transfers between devices: 254 us -> 241 us
  matrix products: 114 us -> 107 us
    all_gather x3 -> x0, waiting for transfers between devices: 83.4 us -> none  [on_device(): normed_rows = lax.all_gather(normed, 'col', axis=0, tiled=True)]
    ppermute x0 -> x9, waiting for transfers between devices: none -> 74.9 us  [on_device(): lax.ppermute(shard, 'col', [(d, (d + 1) % ways) for d in range(ways)])]
    dot_general x3, matrix products: 41.2 us -> 34.8 us  [on_device(): up_part = jnp.dot(normed_rows, up_tile, preferred_element_type=jnp.float32)]
  transfers between devices with their start and end apart: 11 -> 17, of which waited for: 11 -> 17; matrix products, arithmetic and copies ran while one was open for 0% -> 0% of each run, Pallas kernels for 0% -> 0%
where the time goes in v1:
time: 438 us
  waiting for transfers between devices  241 us (55%)
  matrix products  107 us (24%)
  blocking collectives  54 us (12%)
  other arithmetic  15.8 us (4%)
  between operations  13.7 us (3%)
  starting transfers between devices  5.22 us (1%)
    reduce_scatter x3, waiting for transfers between devices, on_device(): lax.psum_scatter(jnp.dot(hidden, down_tile, preferred_element_type=jnp.fl...  82.2 us
    reduce_scatter x3, waiting for transfers between devices, on_device(): lax.psum_scatter(pair.astype(jnp.bfloat16), 'row', scatter_dimension=0, t...  81.9 us
    ppermute x9, waiting for transfers between devices, on_device(): lax.ppermute(shard, 'col', [(d, (d + 1) % ways) for d in range(ways)])  74.9 us
    all_gather x3, blocking collectives, on_device(): hidden = lax.all_gather(hidden_share, 'row', axis=0, tiled=True)  38.3 us
    dot_general x3, matrix products, on_device(): jnp.dot(hidden, down_tile, preferred_element_type=jnp.float32)  37.7 us
    dot_general x3, matrix products, on_device(): up_part = jnp.dot(normed_rows, up_tile, preferred_element_type=jnp.float32)  34.8 us
    dot_general x3, matrix products, on_device(): jnp.dot(normed_rows, gate_tile, preferred_element_type=jnp.float32)  34.8 us
    psum x3, blocking collectives, on_device(): sum_sq = lax.psum(jnp.sum(wide_in * wide_in, axis=1), 'row')  15.7 us
  transfers between devices with their start and end apart: 17, of which 17 were waited for; matrix products, arithmetic and copies ran while one was open for 0% of the time, Pallas kernels for 0%

profile of v1, /device:TPU:0, one launch (start us, length us, event | category | flops | bytes accessed | tf_op | source)
XLA Modules:
  0.0 437.8 jit_solution(18431839533045154283)
XLA Ops:
  7.7 5.9 %psum.21 = f32[32]{0:T(128)S(1)} all-reduce(f32[32]{0:T(128)S(1)} %fusion.56), channel_id=1, replica_groups=mesh['group'=2,'col'=4,'row'=2,'section'=2] {'row'}, use_global_device_ids=true, to_apply=%region_1.2 | all-reduce | flops 32 | bytes 256 | tf_op jit(solution)/shard_map/psum | solution.py:31
  14.7 2.2 collective-permute-start
  16.9 7.2 %collective-permute-done = bf16[32,4096]{1,0:T(8,128)(2,1)S(1)} collective-permute-done((bf16[32,4096]{1,0:T(8,128)(2,1)S(1)}, bf16[32,4096]{1,0:T(8,128)(2,1)S(1)}, u32[]{:S(2)}, u32[]{:S(2)}) %collective-permute-start) | collective-permute-done | bytes 262176 | tf_op jit(solution)/shard_map/ppermute | solution.py:42
  24.1 8.1 %collective-permute-done.1 = bf16[32,4096]{1,0:T(8,128)(2,1)S(1)} collective-permute-done((bf16[32,4096]{1,0:T(8,128)(2,1)S(1)}, bf16[32,4096]{1,0:T(8,128)(2,1)S(1)}, u32[]{:S(2)}, u32[]{:S(2)}) %collective-permute-start.1) | collective-permute-done | bytes 262176 | tf_op jit(solution)/shard_map/ppermute | solution.py:42
  32.3 8.1 %collective-permute-done.2 = bf16[32,4096]{1,0:T(8,128)(2,1)S(1)} collective-permute-done((bf16[32,4096]{1,0:T(8,128)(2,1)S(1)}, bf16[32,4096]{1,0:T(8,128)(2,1)S(1)}, u32[]{:S(2)}, u32[]{:S(2)}) %collective-permute-start.2) | collective-permute-done | bytes 262176 | tf_op jit(solution)/shard_map/ppermute | solution.py:42
  40.5 11.6 %fusion.18 = bf16[128,3584]{1,0:T(8,128)(2,1)S(1)} fusion(bf16[128,4096]{1,0:T(8,128)(2,1)S(1)} %constant_dynamic-update-slice_fusion.8, bf16[1,4096,3584]{2,1,0:T(8,128)(2,1)} %param.7), kind=kOutput, calls=%fused_computation.18 | convolution fusion | flops 3758555136 | bytes 31326208 | tf_op jit(solution)/shard_map/dot_general | solution.py:45
  52.0 11.6 %fusion.27 = bf16[128,3584]{1,0:T(8,128)(2,1)S(1)} fusion(bf16[128,4096]{1,0:T(8,128)(2,1)S(1)} %constant_dynamic-update-slice_fusion.8, bf16[1,4096,3584]{2,1,0:T(8,128)(2,1)} %param.8), kind=kOutput, calls=%fused_computation.21 | convolution fusion | flops 3758555136 | bytes 31326208 | tf_op jit(solution)/shard_map/dot_general | solution.py:46
  63.6 1.4 pad_maximum_fusion
  65.1 27.4 %reduce-scatter.7.cloned.1.call-done = bf16[64,7168]{1,0:T(8,128)(2,1)} async-done(((bf16[128,7168]{1,0:T(8,128)(2,1)}), bf16[64,7168]{1,0:T(8,128)(2,1)}) %reduce-scatter.7.cloned.1.call-update) | async-done | bytes 917520 | tf_op jit(solution)/shard_map/reduce_scatter | solution.py:48
  94.1 12.8 %all_gather.9 = bf16[128,3584]{1,0:T(8,128)(2,1)S(1)} all-gather(bf16[64,3584]{1,0:T(8,128)(2,1)S(1)} %fusion.47), channel_id=1, replica_groups=mesh['group'=2,'col'=4,'row'=2,'section'=2] {'row'}, dimensions={0}, use_global_device_ids=true | all-gather | bytes 1376256 | tf_op jit(solution)/shard_map/all_gather | solution.py:54
  106.8 12.6 %fusion.36 = bf16[128,4096]{1,0:T(8,128)(2,1)} fusion(bf16[128,3584]{1,0:T(8,128)(2,1)S(1)} %all_gather.9, bf16[1,3584,4096]{2,1,0:T(8,128)(2,1)} %param.9), kind=kOutput, calls=%fused_computation.24 | convolution fusion | flops 3758620672 | bytes 31326208 | tf_op jit(solution)/shard_map/dot_general | solution.py:56
  119.5 27.4 %reduce-scatter.9.cloned.1.call-done = bf16[32,4096]{1,0:T(8,128)(2,1)} async-done(((bf16[128,4096]{1,0:T(8,128)(2,1)}), bf16[32,4096]{1,0:T(8,128)(2,1)}) %reduce-scatter.9.cloned.1.call-update) | async-done | bytes 262160 | tf_op jit(solution)/shard_map/reduce_scatter | solution.py:55
  150.6 4.9 %psum.22 = f32[32]{0:T(128)S(1)} all-reduce(f32[32]{0:T(128)S(1)} %get-tuple-element.9), channel_id=1, replica_groups=mesh['group'=2,'col'=4,'row'=2,'section'=2] {'row'}, use_global_device_ids=true, to_apply=%region_5.6 | all-reduce | flops 32 | bytes 256 | tf_op jit(solution)/shard_map/psum | solution.py:31
  155.9 9.2 %collective-permute-done.4 = bf16[32,4096]{1,0:T(8,128)(2,1)S(1)} collective-permute-done((bf16[32,4096]{1,0:T(8,128)(2,1)S(1)}, bf16[32,4096]{1,0:T(8,128)(2,1)S(1)}, u32[]{:S(2)}, u32[]{:S(2)}) %collective-permute-start.4) | collective-permute-done | bytes 262176 | tf_op jit(solution)/shard_map/ppermute | solution.py:42
  165.1 8.3 %collective-permute-done.5 = bf16[32,4096]{1,0:T(8,128)(2,1)S(1)} collective-permute-done((bf16[32,4096]{1,0:T(8,128)(2,1)S(1)}, bf16[32,4096]{1,0:T(8,128)(2,1)S(1)}, u32[]{:S(2)}, u32[]{:S(2)}) %collective-permute-start.5) | collective-permute-done | bytes 262176 | tf_op jit(solution)/shard_map/ppermute | solution.py:42
  173.5 8.1 %collective-permute-done.6 = bf16[32,4096]{1,0:T(8,128)(2,1)S(1)} collective-permute-done((bf16[32,4096]{1,0:T(8,128)(2,1)S(1)}, bf16[32,4096]{1,0:T(8,128)(2,1)S(1)}, u32[]{:S(2)}, u32[]{:S(2)}) %collective-permute-start.6) | collective-permute-done | bytes 262176 | tf_op jit(solution)/shard_map/ppermute | solution.py:42
  181.7 11.6 %fusion.21 = bf16[128,3584]{1,0:T(8,128)(2,1)S(1)} fusion(bf16[128,4096]{1,0:T(8,128)(2,1)S(1)} %constant_dynamic-update-slice_fusion.4, bf16[1,4096,3584]{2,1,0:T(8,128)(2,1)} %param.7), kind=kOutput, calls=%fused_computation.19 | convolution fusion | flops 3758555136 | bytes 31326208 | tf_op jit(solution)/shard_map/dot_general | solution.py:45
  193.3 11.6 %fusion.30 = bf16[128,3584]{1,0:T(8,128)(2,1)S(1)} fusion(bf16[128,4096]{1,0:T(8,128)(2,1)S(1)} %constant_dynamic-update-slice_fusion.4, bf16[1,4096,3584]{2,1,0:T(8,128)(2,1)} %param.8), kind=kOutput, calls=%fused_computation.22 | convolution fusion | flops 3758555136 | bytes 31326208 | tf_op jit(solution)/shard_map/dot_general | solution.py:46
  206.4 27.3 %reduce-scatter.11.cloned.1.call-done = bf16[64,7168]{1,0:T(8,128)(2,1)} async-done(((bf16[128,7168]{1,0:T(8,128)(2,1)}), bf16[64,7168]{1,0:T(8,128)(2,1)}) %reduce-scatter.11.cloned.1.call-update) | async-done | bytes 917520 | tf_op jit(solution)/shard_map/reduce_scatter | solution.py:48
  235.2 12.8 %all_gather.10 = bf16[128,3584]{1,0:T(8,128)(2,1)S(1)} all-gather(bf16[64,3584]{1,0:T(8,128)(2,1)S(1)} %fusion.46), channel_id=1, replica_groups=mesh['group'=2,'col'=4,'row'=2,'section'=2] {'row'}, dimensions={0}, use_global_device_ids=true | all-gather | bytes 1376256 | tf_op jit(solution)/shard_map/all_gather | solution.py:54
  248.0 12.5 %fusion.39 = bf16[128,4096]{1,0:T(8,128)(2,1)} fusion(bf16[128,3584]{1,0:T(8,128)(2,1)S(1)} %all_gather.10, bf16[1,3584,4096]{2,1,0:T(8,128)(2,1)} %param.9), kind=kOutput, calls=%fused_computation.25 | convolution fusion | flops 3758620672 | bytes 31326208 | tf_op jit(solution)/shard_map/dot_general | solution.py:56
  260.6 27.4 %reduce-scatter.13.cloned.1.call-done = bf16[32,4096]{1,0:T(8,128)(2,1)} async-done(((bf16[128,4096]{1,0:T(8,128)(2,1)}), bf16[32,4096]{1,0:T(8,128)(2,1)}) %reduce-scatter.13.cloned.1.call-update) | async-done | bytes 262160 | tf_op jit(solution)/shard_map/reduce_scatter | solution.py:55
  291.7 4.9 %psum.23 = f32[32]{0:T(128)S(1)} all-reduce(f32[32]{0:T(128)S(1)} %fusion.52), channel_id=1, replica_groups=mesh['group'=2,'col'=4,'row'=2,'section'=2] {'row'}, use_global_device_ids=true, to_apply=%region_9.10 | all-reduce | flops 32 | bytes 256 | tf_op jit(solution)/shard_map/psum | solution.py:31
  297.0 9.2 %collective-permute-done.8 = bf16[32,4096]{1,0:T(8,128)(2,1)S(1)} collective-permute-done((bf16[32,4096]{1,0:T(8,128)(2,1)S(1)}, bf16[32,4096]{1,0:T(8,128)(2,1)S(1)}, u32[]{:S(2)}, u32[]{:S(2)}) %collective-permute-start.8) | collective-permute-done | bytes 262176 | tf_op jit(solution)/shard_map/ppermute | solution.py:42
  306.2 8.3 %collective-permute-done.9 = bf16[32,4096]{1,0:T(8,128)(2,1)S(1)} collective-permute-done((bf16[32,4096]{1,0:T(8,128)(2,1)S(1)}, bf16[32,4096]{1,0:T(8,128)(2,1)S(1)}, u32[]{:S(2)}, u32[]{:S(2)}) %collective-permute-start.9) | collective-permute-done | bytes 262176 | tf_op jit(solution)/shard_map/ppermute | solution.py:42
  314.6 8.1 %collective-permute-done.10 = bf16[32,4096]{1,0:T(8,128)(2,1)S(1)} collective-permute-done((bf16[32,4096]{1,0:T(8,128)(2,1)S(1)}, bf16[32,4096]{1,0:T(8,128)(2,1)S(1)}, u32[]{:S(2)}, u32[]{:S(2)}) %collective-permute-start.10) | collective-permute-done | bytes 262176 | tf_op jit(solution)/shard_map/ppermute | solution.py:42
  322.7 11.6 %fusion.24 = bf16[128,3584]{1,0:T(8,128)(2,1)S(1)} fusion(bf16[128,4096]{1,0:T(8,128)(2,1)S(1)} %constant_dynamic-update-slice_fusion, bf16[1,4096,3584]{2,1,0:T(8,128)(2,1)} %param.7), kind=kOutput, calls=%fused_computation.20 | convolution fusion | flops 3758555136 | bytes 31326208 | tf_op jit(solution)/shard_map/dot_general | solution.py:45
  334.3 11.6 %fusion.33 = bf16[128,3584]{1,0:T(8,128)(2,1)S(1)} fusion(bf16[128,4096]{1,0:T(8,128)(2,1)S(1)} %constant_dynamic-update-slice_fusion, bf16[1,4096,3584]{2,1,0:T(8,128)(2,1)} %param.8), kind=kOutput, calls=%fused_computation.23 | convolution fusion | flops 3758555136 | bytes 31326208 | tf_op jit(solution)/shard_map/dot_general | solution.py:46
  347.5 27.3 %reduce-scatter.15.cloned.1.call-done = bf16[64,7168]{1,0:T(8,128)(2,1)} async-done(((bf16[128,7168]{1,0:T(8,128)(2,1)}), bf16[64,7168]{1,0:T(8,128)(2,1)}) %reduce-scatter.15.cloned.1.call-update) | async-done | bytes 917520 | tf_op jit(solution)/shard_map/reduce_scatter | solution.py:48
  376.3 12.8 %all_gather.11 = bf16[128,3584]{1,0:T(8,128)(2,1)S(1)} all-gather(bf16[64,3584]{1,0:T(8,128)(2,1)S(1)} %fusion.45), channel_id=1, replica_groups=mesh['group'=2,'col'=4,'row'=2,'section'=2] {'row'}, dimensions={0}, use_global_device_ids=true | all-gather | bytes 1376256 | tf_op jit(solution)/shard_map/all_gather | solution.py:54
  389.1 12.5 %fusion.42 = bf16[128,4096]{1,0:T(8,128)(2,1)} fusion(bf16[128,3584]{1,0:T(8,128)(2,1)S(1)} %all_gather.11, bf16[1,3584,4096]{2,1,0:T(8,128)(2,1)} %param.9), kind=kOutput, calls=%fused_computation.26 | convolution fusion | flops 3758620672 | bytes 31326208 | tf_op jit(solution)/shard_map/dot_general | solution.py:56
  401.6 27.4 %reduce-scatter.17.cloned.1.call-done = bf16[32,4096]{1,0:T(8,128)(2,1)} async-done(((bf16[128,4096]{1,0:T(8,128)(2,1)}), bf16[32,4096]{1,0:T(8,128)(2,1)}) %reduce-scatter.17.cloned.1.call-update) | async-done | bytes 262160 | tf_op jit(solution)/shard_map/reduce_scatter | solution.py:55
  (61 shorter events, 20.3 us)
Async XLA Ops:
  6.5 86.0 %reduce-scatter.7.cloned.1.call-start = ((), (), s32[]{:S(2)}) async-start(), calls=%async_computation.6 | async-start | bytes 2752512 | tf_op jit(solution)/shard_map/reduce_scatter | solution.py:48
  14.7 9.3 %collective-permute-start = (bf16[32,4096]{1,0:T(8,128)(2,1)S(1)}, bf16[32,4096]{1,0:T(8,128)(2,1)S(1)}, u32[]{:S(2)}, u32[]{:S(2)}) collective-permute-start(bf16[32,4096]{1,0:T(8,128)(2,1)S(1)} %get-tuple-element.12), channel_id=1, source_target_pairs={{0,4},{4,8},{8,12},{12,0},{1,5},{5,9},{9,13},{13,1},{2,6},{6,10},{... | collective-permute-start | bytes 786440 | tf_op jit(solution)/shard_map/ppermute | solution.py:42
  24.1 8.2 %collective-permute-start.1 = (bf16[32,4096]{1,0:T(8,128)(2,1)S(1)}, bf16[32,4096]{1,0:T(8,128)(2,1)S(1)}, u32[]{:S(2)}, u32[]{:S(2)}) collective-permute-start(bf16[32,4096]{1,0:T(8,128)(2,1)S(1)} %collective-permute-done), channel_id=1, source_target_pairs={{0,4},{4,8},{8,12},{12,0},{1,5},{5,9},{9,13},{13,1},{2,6},{6,10},{... | collective-permute-start | bytes 786440 | tf_op jit(solution)/shard_map/ppermute | solution.py:42
  32.3 8.2 %collective-permute-start.2 = (bf16[32,4096]{1,0:T(8,128)(2,1)S(1)}, bf16[32,4096]{1,0:T(8,128)(2,1)S(1)}, u32[]{:S(2)}, u32[]{:S(2)}) collective-permute-start(bf16[32,4096]{1,0:T(8,128)(2,1)S(1)} %collective-permute-done.1), channel_id=1, source_target_pairs={{0,4},{4,8},{8,12},{12,0},{1,5},{5,9},{9,13},{13,1},{2,6},{6,10},{... | collective-permute-start | bytes 786440 | tf_op jit(solution)/shard_map/ppermute | solution.py:42
  65.1 81.8 %reduce-scatter.9.cloned.1.call-start = ((), (), s32[]{:S(2)}) async-start(), calls=%async_computation.7 | async-start | bytes 1310720 | tf_op jit(solution)/shard_map/reduce_scatter | solution.py:55
  106.8 40.1 %copy-start = (bf16[2,32,4096]{2,1,0:T(8,128)(2,1)S(1)}, bf16[2,32,4096]{2,1,0:T(8,128)(2,1)}, u32[]{:S(2)}) copy-start(bf16[2,32,4096]{2,1,0:T(8,128)(2,1)} %param.5) | copy-start | bytes 1572868
  119.4 36.3 %copy-start.1 = (f32[1,4096]{1,0:T(1,128)S(1)}, f32[1,4096]{1,0:T(1,128)}, u32[]{:S(2)}) copy-start(f32[1,4096]{1,0:T(1,128)} %param.6) | copy-start | bytes 49156
  119.4 114.2 %reduce-scatter.11.cloned.1.call-start = ((), (), s32[]{:S(2)}) async-start(), calls=%async_computation.8 | async-start | bytes 2752512 | tf_op jit(solution)/shard_map/reduce_scatter | solution.py:48
  147.9 2.5 collective-permute-start.3
  155.8 9.3 %collective-permute-start.4 = (bf16[32,4096]{1,0:T(8,128)(2,1)S(1)}, bf16[32,4096]{1,0:T(8,128)(2,1)S(1)}, u32[]{:S(2)}, u32[]{:S(2)}) collective-permute-start(bf16[32,4096]{1,0:T(8,128)(2,1)S(1)} %get-tuple-element.8), channel_id=1, source_target_pairs={{0,4},{4,8},{8,12},{12,0},{1,5},{5,9},{9,13},{13,1},{2,6},{6,10},{... | collective-permute-start | bytes 786440 | tf_op jit(solution)/shard_map/ppermute | solution.py:42
  165.1 8.4 %collective-permute-start.5 = (bf16[32,4096]{1,0:T(8,128)(2,1)S(1)}, bf16[32,4096]{1,0:T(8,128)(2,1)S(1)}, u32[]{:S(2)}, u32[]{:S(2)}) collective-permute-start(bf16[32,4096]{1,0:T(8,128)(2,1)S(1)} %collective-permute-done.4), channel_id=1, source_target_pairs={{0,4},{4,8},{8,12},{12,0},{1,5},{5,9},{9,13},{13,1},{2,6},{6,10},{... | collective-permute-start | bytes 786440 | tf_op jit(solution)/shard_map/ppermute | solution.py:42
  173.5 8.2 %collective-permute-start.6 = (bf16[32,4096]{1,0:T(8,128)(2,1)S(1)}, bf16[32,4096]{1,0:T(8,128)(2,1)S(1)}, u32[]{:S(2)}, u32[]{:S(2)}) collective-permute-start(bf16[32,4096]{1,0:T(8,128)(2,1)S(1)} %collective-permute-done.5), channel_id=1, source_target_pairs={{0,4},{4,8},{8,12},{12,0},{1,5},{5,9},{9,13},{13,1},{2,6},{6,10},{... | collective-permute-start | bytes 786440 | tf_op jit(solution)/shard_map/ppermute | solution.py:42
  206.3 81.7 %reduce-scatter.13.cloned.1.call-start = ((), (), s32[]{:S(2)}) async-start(), calls=%async_computation.9 | async-start | bytes 1310720 | tf_op jit(solution)/shard_map/reduce_scatter | solution.py:55
  260.6 114.2 %reduce-scatter.15.cloned.1.call-start = ((), (), s32[]{:S(2)}) async-start(), calls=%async_computation.10 | async-start | bytes 2752512 | tf_op jit(solution)/shard_map/reduce_scatter | solution.py:48
  289.0 2.5 collective-permute-start.7
  296.9 9.3 %collective-permute-start.8 = (bf16[32,4096]{1,0:T(8,128)(2,1)S(1)}, bf16[32,4096]{1,0:T(8,128)(2,1)S(1)}, u32[]{:S(2)}, u32[]{:S(2)}) collective-permute-start(bf16[32,4096]{1,0:T(8,128)(2,1)S(1)} %get-tuple-element.6), channel_id=1, source_target_pairs={{0,4},{4,8},{8,12},{12,0},{1,5},{5,9},{9,13},{13,1},{2,6},{6,10},{... | collective-permute-start | bytes 786440 | tf_op jit(solution)/shard_map/ppermute | solution.py:42
  306.2 8.4 %collective-permute-start.9 = (bf16[32,4096]{1,0:T(8,128)(2,1)S(1)}, bf16[32,4096]{1,0:T(8,128)(2,1)S(1)}, u32[]{:S(2)}, u32[]{:S(2)}) collective-permute-start(bf16[32,4096]{1,0:T(8,128)(2,1)S(1)} %collective-permute-done.8), channel_id=1, source_target_pairs={{0,4},{4,8},{8,12},{12,0},{1,5},{5,9},{9,13},{13,1},{2,6},{6,10},{... | collective-permute-start | bytes 786440 | tf_op jit(solution)/shard_map/ppermute | solution.py:42
  314.5 8.2 %collective-permute-start.10 = (bf16[32,4096]{1,0:T(8,128)(2,1)S(1)}, bf16[32,4096]{1,0:T(8,128)(2,1)S(1)}, u32[]{:S(2)}, u32[]{:S(2)}) collective-permute-start(bf16[32,4096]{1,0:T(8,128)(2,1)S(1)} %collective-permute-done.9), channel_id=1, source_target_pairs={{0,4},{4,8},{8,12},{12,0},{1,5},{5,9},{9,13},{13,1},{2,6},{6,10},{... | collective-permute-start | bytes 786440 | tf_op jit(solution)/shard_map/ppermute | solution.py:42
  347.4 81.6 %reduce-scatter.17.cloned.1.call-start = ((), (), s32[]{:S(2)}) async-start(), calls=%async_computation.11 | async-start | bytes 1310720 | tf_op jit(solution)/shard_map/reduce_scatter | solution.py:55
Sparse Core Ops, SparseCore 0:
  65.2 27.2 reduce-scatter.6
  119.6 27.3 reduce-scatter.8
  206.5 27.1 reduce-scatter.10
  260.7 27.2 reduce-scatter.12
  347.5 27.1 reduce-scatter.14
  401.7 27.2 reduce-scatter.16
